TPU v7x, 32 devices: a whole 2x2x4 slice. The times are simulated.
32 devices in a mesh: expert: 16 (over z, y, x), dp: 2 (over core).
Axes of the slice: x: 2, y: 2, z: 4, core: 2. Of those that a mesh axis runs over, the one named last changes fastest.
Arguments:
- tokens: bfloat16 [2, 256, 4096], P(None, ('expert', 'dp')), may hold values from -6 to 6
- norm_gain: float32 [4096], replicated, may hold values from 0.5 to 1.5
- route_ids: int32 [2, 256, 8], P(None, ('expert', 'dp')), may hold values from 0 to 15, all different within a row; in each aligned block of 8 rows (0 to 7, 8 to 15, ..., all dimensions but the last counted through in order) at most 8 rows name the same one
- route_weights: float32 [2, 256, 8], P(None, ('expert', 'dp')), may hold values from 0.05 to 0.25
- rows_left: int32 [256], P(('expert', 'dp')), may hold values from 1 to 40
- gate_up_elems: bfloat16 [16, 2, 4096, 1024], P('expert', None, None, 'dp'), may hold values from -0.09375 to 0.09375
- gate_up_scales: bfloat16 [16, 2, 128, 1024], P('expert', None, None, 'dp'), may hold values from 0.5 to 2, as said below
- down_elems: bfloat16 [16, 1024, 4096], P('expert', 'dp'), may hold values from -0.1875 to 0.1875
- down_scales: bfloat16 [16, 32, 4096], P('expert', 'dp'), may hold values from 0.5 to 2, as said below
- swap_pairs: int32 [8], replicated, may hold values 0 or 1
Outputs:
- mixed: bfloat16 [2, 256, 4096], P(None, ('expert', 'dp'))
- new_gate_up_elems: bfloat16 [16, 2, 4096, 1024], P('expert', None, None, 'dp')
- new_gate_up_scales: bfloat16 [16, 2, 128, 1024], P('expert', None, None, 'dp')
- new_down_elems: bfloat16 [16, 1024, 4096], P('expert', 'dp')
- new_down_scales: bfloat16 [16, 32, 4096], P('expert', 'dp')
Inputs may be any that keep to these rules, and one draw needn't show every extreme that they name: `route_ids`: within a step each row names 8 different experts; among the 8 rows of one device in a step, at most 8 name any one expert, and exactly 8 do for some expert. `gate_up_scales`: every entry is a power of two. `down_scales`: every entry is a power of two.
All inputs are finite; a program needn't handle non-finite values.
Results may differ from a plain program's by a relative error of at most 0.0077.
Values may be sent and summed in bfloat16 or wider, within the bound.
No kernel may reach another device: no remote copies, remote signals or barrier semaphores. Data moves between devices by JAX's collectives and lax.ppermute only.
A program may use at most 128 MiB of HBM per device.

v0:
```python
import jax
import jax.numpy as jnp
from jax import lax
from jax.sharding import PartitionSpec as P

mx_block = 32


def partner(x, axis, distance):
    return lax.ppermute(x, axis, [(i, i ^ 1 << distance) for i in range(lax.axis_size(axis))])


def dequantize(elems, scales, axis):
    return elems * jnp.repeat(scales, mx_block, axis=axis)


def rms_normed(rows, norm_gain):
    values = rows.astype(jnp.float32)
    factor = lax.rsqrt(jnp.mean(values * values, axis=-1, keepdims=True) + 1e-06)
    return (values * factor * norm_gain).astype(jnp.bfloat16)


def expert_hidden(rows, gate_up):
    both = jnp.einsum("rd,gdf->grf", rows, gate_up, preferred_element_type=jnp.float32)
    return (jax.nn.silu(both[0]) * both[1]).astype(jnp.bfloat16)


def on_device(
    tokens,
    norm_gain,
    route_ids,
    route_weights,
    rows_left,
    gate_up_elems,
    gate_up_scales,
    down_elems,
    down_scales,
    swap_pairs,
):
    slots = lax.axis_size("expert")
    half = slots // 2
    steps, rows, width = tokens.shape
    top = route_ids.shape[2]
    cap = max(2, min(rows, 2 * rows * top // slots))
    here = lax.axis_index("expert")
    pair_iota = jnp.arange(half, dtype=jnp.int32)
    slot_iota = jnp.arange(slots, dtype=jnp.int32)
    own_flag = jnp.sum(jnp.where(pair_iota == here % half, swap_pairs, 0))
    initial = (gate_up_elems, gate_up_scales, down_elems, down_scales)
    swapped = initial
    results = []
    for step in range(steps):
        if step == steps // 2:
            received = partner(
                (gate_up_elems, gate_up_scales, down_elems, down_scales),
                "expert",
                slots.bit_length() - 2,
            )
            swapped = tuple(
                (jnp.where(own_flag > 0, other, mine) for mine, other in zip(initial, received))
            )
        ids = route_ids[step]
        normed = rms_normed(tokens[step], norm_gain)
        live = rows_left > step
        flat_live = jnp.repeat(live, top)
        flat_dest = ids.reshape(-1)
        hits = ((flat_dest[:, None] == slot_iota[None, :]) & flat_live[:, None]).astype(jnp.int32)
        rank = jnp.sum(jnp.cumsum(hits, axis=0) * hits, axis=1) - 1
        slot_index = jnp.where(flat_live, flat_dest * cap + rank, slots * cap)
        sources = jnp.repeat(normed, top, axis=0)
        send = (
            jnp.zeros((slots * cap, width), jnp.bfloat16)
            .at[slot_index]
            .set(sources, mode="drop")
            .reshape(slots, cap, width)
        )
        gate_up = dequantize(initial[0][0], initial[1][0], 1)
        down = dequantize(initial[2][0], initial[3][0], 0)
        arrived = lax.all_to_all(send, "expert", split_axis=0, concat_axis=0, tiled=True)
        piece = lax.all_gather(arrived, "dp", axis=0, tiled=True)
        flat = piece.reshape(-1, width)
        hidden = expert_hidden(flat, gate_up).reshape(piece.shape[0], piece.shape[1], -1)
        hidden_rows = hidden.reshape(-1, hidden.shape[2])
        summed = lax.psum_scatter(
            jnp.dot(hidden_rows, down, preferred_element_type=jnp.float32).astype(jnp.bfloat16),
            "dp",
            scatter_dimension=0,
            tiled=True,
        )
        result = summed.reshape(slots, cap, width)
        back = lax.all_to_all(result, "expert", split_axis=0, concat_axis=0, tiled=True)
        picked = back.reshape(-1, width)[jnp.minimum(slot_index, slots * cap - 1)]
        factor = route_weights[step].reshape(-1) * flat_live.astype(jnp.float32)
        mixed_step = jnp.sum(
            (picked.astype(jnp.float32) * factor[:, None]).reshape(rows, top, width), axis=1
        )
        results.append(mixed_step.astype(jnp.bfloat16))
    mixed = jnp.stack(results)
    return (mixed, swapped[0], swapped[1], swapped[2], swapped[3])


def solution(mesh):
    in_specs = (
        P(None, ("expert", "dp"), None),
        P(),
        P(None, ("expert", "dp"), None),
        P(None, ("expert", "dp"), None),
        P(("expert", "dp")),
        P("expert", None, None, "dp"),
        P("expert", None, None, "dp"),
        P("expert", "dp", None),
        P("expert", "dp", None),
        P(),
    )
    out_specs = (
        P(None, ("expert", "dp"), None),
        P("expert", None, None, "dp"),
        P("expert", None, None, "dp"),
        P("expert", "dp", None),
        P("expert", "dp", None),
    )
    return jax.shard_map(
        on_device, mesh=mesh, in_specs=in_specs, out_specs=out_specs, check_vma=False
    )
```

profile of v0, /device:TPU:17, one launch (start us, length us, event | category | flops | bytes accessed | tf_op | source)
XLA Modules:
  0.0 702.7 jit_solution(17926109491885856133)
XLA Ops:
  7.2 0.7 broadcast_compare_fusion.1
  7.8 0.1 broadcast_in_dim.20
  7.9 0.1 and.26
  8.0 0.1 reshape.274
  8.1 0.7 fusion.57
  8.8 0.1 eq.38
  8.9 0.1 fusion.43
  9.0 0.1 reduce_window_sum.17
  9.1 0.2 select_reduce_fusion.1
  9.3 0.1 mul.136
  9.4 1.0 fusion.36
  10.4 1.0 fusion.38
  11.4 2.4 scatter_custom_fusion
  13.8 6.6 all-to-all-start
  20.4 0.0 all-gather.3.cloned.1.call-start
  20.4 0.2 collective-permute-start.2
  20.6 0.1 broadcast_in_dim.44
  20.7 0.1 and.29
  20.8 0.1 reshape.281
  20.8 0.1 eq.42
  20.9 0.1 fusion.45
  21.0 0.1 reduce_window_sum.18
  21.1 0.1 mul.151
  21.2 0.2 select_reduce_fusion
  21.4 112.9 %all-to-all-done = bf16[16,8,4096]{2,1,0:T(8,128)(2,1)S(1)} async-done(((bf16[16,8,4096]{2,1,0:T(8,128)(2,1)}), bf16[16,8,4096]{2,1,0:T(8,128)(2,1)S(1)}, u32[]{:S(2)}, u32[]{:S(2)}) %all-to-all-start) | async-done | bytes 1048608 | tf_op jit(solution)/shard_map/all_to_all | solution.py:79
  134.3 1.0 copy-done.1
  135.3 2.4 scatter_custom_fusion.1
  137.7 4.8 all-to-all-start.2
  142.5 0.0 all-gather.5.cloned.1.call-start
  142.6 0.6 fusion.46
  143.9 102.8 %all-to-all-done.2 = bf16[16,8,4096]{2,1,0:T(8,128)(2,1)S(1)} async-done(((bf16[16,8,4096]{2,1,0:T(8,128)(2,1)}), bf16[16,8,4096]{2,1,0:T(8,128)(2,1)S(1)}, u32[]{:S(2)}, u32[]{:S(2)}) %all-to-all-start.2) | async-done | bytes 1048608 | tf_op jit(solution)/shard_map/all_to_all | solution.py:79
  246.7 1.0 copy-done.2
  247.7 0.0 reduce-scatter.3.cloned.1.call-start
  247.8 0.0 all-gather.3.cloned.1.call-done
  247.8 0.7 broadcast_in_dim.19
  248.5 0.9 copy-done.9
  249.4 8.1 %fusion.10 = f32[2,256,512]{1,2,0:T(8,128)S(1)} fusion(bf16[32,8,4096]{2,1,0:T(8,128)(2,1)S(1)} %copy-done.9, bf16[1,2,4096,512]{3,2,1,0:T(8,128)(2,1)} %param.15, bf16[1,2,4096,512]{3,2,1,0:T(8,128)(2,1)S(1)} %bitcast.100), kind=kOutput, calls=%fused_computation.19 | convolution fusion | flops 2151677952 | bytes 19922944 | tf_op jit(solution)/shard_map/rd,gdf->grf/dot_general | solution.py:24
  257.5 0.5 broadcast_in_dim.23
  258.0 1.9 copy-done.3
  260.0 2.5 broadcast_select_fusion.1
  262.5 2.0 copy-done.4
  264.4 2.7 convolution_convert_fusion.1
  267.1 0.2 reduce-scatter.5.cloned.1.call-start
  267.4 0.1 collective-permute-start
  267.4 0.0 all-gather.5.cloned.1.call-done
  267.5 9.0 %fusion.15 = f32[2,256,512]{1,2,0:T(8,128)S(1)} fusion(bf16[32,8,4096]{2,1,0:T(8,128)(2,1)} %all-gather.5.cloned.1.call-done, bf16[1,2,4096,512]{3,2,1,0:T(8,128)(2,1)} %param.15, bf16[1,2,4096,512]{3,2,1,0:T(8,128)(2,1)} %bitcast.101), kind=kOutput, calls=%fused_computation.20 | convolution fusion | flops 2151677952 | bytes 19922944 | tf_op jit(solution)/shard_map/rd,gdf->grf/dot_general | solution.py:24
  276.6 2.7 convolution_convert_fusion
  279.3 0.8 reduce-scatter.3.cloned.1.call-done
  280.1 7.7 %all-to-all-start.1 = ((bf16[16,8,4096]{2,1,0:T(8,128)(2,1)}), bf16[16,8,4096]{2,1,0:T(8,128)(2,1)S(1)}, u32[]{:S(2)}, u32[]{:S(2)}) async-start(bf16[16,8,4096]{2,1,0:T(8,128)(2,1)} %bitcast.103), calls=%async_computation.2 | async-start | bytes 2097152 | tf_op jit(solution)/shard_map/all_to_all | solution.py:91
  287.8 0.2 collective-permute-start.1
  287.9 2.2 collective-permute-start.3
  290.1 0.1 bitcast_select_fusion.1
  290.2 4.7 reduce-scatter.5.cloned.1.call-done
  294.9 367.7 %all-to-all-done.1 = bf16[16,8,4096]{2,1,0:T(8,128)(2,1)S(1)} async-done(((bf16[16,8,4096]{2,1,0:T(8,128)(2,1)}), bf16[16,8,4096]{2,1,0:T(8,128)(2,1)S(1)}, u32[]{:S(2)}, u32[]{:S(2)}) %all-to-all-start.1) | async-done | bytes 1048608 | tf_op jit(solution)/shard_map/all_to_all | solution.py:91
  662.7 4.9 all-to-all-start.3
  667.6 0.7 broadcast_select_fusion.3
  668.2 0.7 broadcast_select_fusion.2
  669.0 7.3 %broadcast_select_fusion = bf16[1,2,4096,512]{3,2,1,0:T(8,128)(2,1)} fusion(bf16[1,2,4096,512]{3,2,1,0:T(8,128)(2,1)} %collective-permute-done, bf16[1,2,4096,512]{3,2,1,0:T(8,128)(2,1)} %param.15, pred[]{:T(512)S(6)} %gt.14), kind=kLoop, calls=%fused_computation.8 | loop fusion | flops 4194304 | bytes 25165824 | tf_op jit(solution)/shard_map/jit(_where)/select_n | solution.py:60
  676.2 0.9 gather_fusion
  677.1 0.5 fusion.21
  677.6 16.6 %all-to-all-done.3 = bf16[16,8,4096]{2,1,0:T(8,128)(2,1)S(1)} async-done(((bf16[16,8,4096]{2,1,0:T(8,128)(2,1)}), bf16[16,8,4096]{2,1,0:T(8,128)(2,1)S(1)}, u32[]{:S(2)}, u32[]{:S(2)}) %all-to-all-start.3) | async-done | bytes 1048608 | tf_op jit(solution)/shard_map/all_to_all | solution.py:91
  694.1 0.9 gather_fusion.1
  695.0 0.5 fusion.20
  695.5 0.7 pad_maximum_fusion
  (32 shorter events, 0.2 us)
Async XLA Ops:
  7.2 135.4 %copy-start.10 = (s32[8]{0:T(128)S(1)}, s32[8]{0:T(128)}, u32[]{:S(2)}) copy-start(s32[8]{0:T(128)} %param.19) | copy-start | bytes 100
  11.4 236.4 %copy-start.6 = (bf16[1,2,128,512]{3,2,1,0:T(8,128)(2,1)S(1)}, bf16[1,2,128,512]{3,2,1,0:T(8,128)(2,1)}, u32[]{:S(2)}) copy-start(bf16[1,2,128,512]{3,2,1,0:T(8,128)(2,1)} %param.16) | copy-start | bytes 786436
  13.8 120.4 %all-to-all-start = ((bf16[16,8,4096]{2,1,0:T(8,128)(2,1)}), bf16[16,8,4096]{2,1,0:T(8,128)(2,1)S(1)}, u32[]{:S(2)}, u32[]{:S(2)}) async-start(bf16[16,8,4096]{2,1,0:T(8,128)(2,1)} %bitcast.8), calls=%async_computation | async-start | bytes 2097152 | tf_op jit(solution)/shard_map/all_to_all | solution.py:79
  20.4 227.4 %all-gather.3.cloned.1.call-start = ((), (), s32[]{:S(2)}) async-start(), calls=%async_computation.6 | async-start | bytes 3145728 | tf_op jit(solution)/shard_map/all_gather | solution.py:80
  20.4 237.1 %collective-permute-start.2 = (bf16[1,512,4096]{2,1,0:T(8,128)(2,1)}, bf16[1,512,4096]{2,1,0:T(8,128)(2,1)}, u32[]{:S(2)}, u32[]{:S(2)}) collective-permute-start(bf16[1,512,4096]{2,1,0:T(8,128)(2,1)} %param.17), channel_id=1, source_target_pairs={{0,16},{2,18},{4,20},{6,22},{8,24},{10,26},{12,28},{14,30},{16,0},... | collective-permute-start | bytes 12582920 | tf_op jit(solution)/shard_map/ppermute | solution.py:10
  134.3 1.0 copy-start.1
  137.7 109.0 %all-to-all-start.2 = ((bf16[16,8,4096]{2,1,0:T(8,128)(2,1)}), bf16[16,8,4096]{2,1,0:T(8,128)(2,1)S(1)}, u32[]{:S(2)}, u32[]{:S(2)}) async-start(bf16[16,8,4096]{2,1,0:T(8,128)(2,1)} %bitcast.27), calls=%async_computation.3 | async-start | bytes 2097152 | tf_op jit(solution)/shard_map/all_to_all | solution.py:79
  142.5 124.9 %all-gather.5.cloned.1.call-start = ((), (), s32[]{:S(2)}) async-start(), calls=%async_computation.8 | async-start | bytes 3145728 | tf_op jit(solution)/shard_map/all_gather | solution.py:80
  246.7 1.0 copy-start.2
  247.7 32.4 %reduce-scatter.3.cloned.1.call-start = ((), (), s32[]{:S(2)}) async-start(), calls=%async_computation.7 | async-start | bytes 3145728 | tf_op jit(solution)/shard_map/reduce_scatter | solution.py:84
  247.8 1.6 copy-start.9
  248.5 9.0 %copy-start = (bf16[2,128,32,512]{3,2,1,0:T(8,128)(2,1)}, bf16[2,128,32,512]{3,2,1,0:T(8,128)(2,1)S(1)}, u32[]{:S(2)}) copy-start(bf16[2,128,32,512]{3,2,1,0:T(8,128)(2,1)S(1)} %broadcast_in_dim.19) | copy-start | bytes 25165828
  249.4 8.1 %copy-start.7 = (bf16[1,16,4096]{2,1,0:T(8,128)(2,1)S(1)}, bf16[1,16,4096]{2,1,0:T(8,128)(2,1)}, u32[]{:S(2)}) copy-start(bf16[1,16,4096]{2,1,0:T(8,128)(2,1)} %param.18) | copy-start | bytes 393220
  257.5 2.5 copy-start.3
  262.5 2.0 copy-start.4
  267.1 27.8 %reduce-scatter.5.cloned.1.call-start = ((), (), s32[]{:S(2)}) async-start(), calls=%async_computation.9 | async-start | bytes 3145728 | tf_op jit(solution)/shard_map/reduce_scatter | solution.py:84
  267.4 401.6 %collective-permute-start = (bf16[1,2,4096,512]{3,2,1,0:T(8,128)(2,1)}, bf16[1,2,4096,512]{3,2,1,0:T(8,128)(2,1)}, u32[]{:S(2)}, u32[]{:S(2)}) collective-permute-start(bf16[1,2,4096,512]{3,2,1,0:T(8,128)(2,1)} %param.15), channel_id=1, source_target_pairs={{0,16},{2,18},{4,20},{6,22},{8,24},{10,26},{12,28},{14,30},{16,0},... | collective-permute-start | bytes 25165832 | tf_op jit(solution)/shard_map/ppermute | solution.py:10
  267.5 9.1 %copy-start.5 = (bf16[1,512,4096]{2,1,0:T(8,128)(2,1)S(1)}, bf16[1,512,4096]{2,1,0:T(8,128)(2,1)}, u32[]{:S(2)}) copy-start(bf16[1,512,4096]{2,1,0:T(8,128)(2,1)} %copy-done.4) | copy-start | bytes 12582916
  276.5 13.6 %copy-start.8 = (f32[2,8,8]{2,1,0:T(8,128)S(1)}, f32[2,8,8]{2,1,0:T(8,128)}, u32[]{:S(2)}) copy-start(f32[2,8,8]{2,1,0:T(8,128)} %param.13) | copy-start | bytes 1540
  280.1 382.6 %all-to-all-start.1 = ((bf16[16,8,4096]{2,1,0:T(8,128)(2,1)}), bf16[16,8,4096]{2,1,0:T(8,128)(2,1)S(1)}, u32[]{:S(2)}, u32[]{:S(2)}) async-start(bf16[16,8,4096]{2,1,0:T(8,128)(2,1)} %bitcast.103), calls=%async_computation.2 | async-start | bytes 2097152 | tf_op jit(solution)/shard_map/all_to_all | solution.py:91
  287.8 380.4 %collective-permute-start.1 = (bf16[1,2,128,512]{3,2,1,0:T(8,128)(2,1)S(1)}, bf16[1,2,128,512]{3,2,1,0:T(8,128)(2,1)S(1)}, u32[]{:S(2)}, u32[]{:S(2)}) collective-permute-start(bf16[1,2,128,512]{3,2,1,0:T(8,128)(2,1)S(1)} %copy-done.6), channel_id=1, source_target_pairs={{0,16},{2,18},{4,20},{6,22},{8,24},{10,26},{12,28},{14,30},{16,0},... | collective-permute-start | bytes 786440 | tf_op jit(solution)/shard_map/ppermute | solution.py:10
  287.9 379.6 %collective-permute-start.3 = (bf16[1,16,4096]{2,1,0:T(8,128)(2,1)S(1)}, bf16[1,16,4096]{2,1,0:T(8,128)(2,1)S(1)}, u32[]{:S(2)}, u32[]{:S(2)}) collective-permute-start(bf16[1,16,4096]{2,1,0:T(8,128)(2,1)S(1)} %copy-done.7), channel_id=1, source_target_pairs={{0,16},{2,18},{4,20},{6,22},{8,24},{10,26},{12,28},{14,30},{16,0},... | collective-permute-start | bytes 393224 | tf_op jit(solution)/shard_map/ppermute | solution.py:10
  662.7 31.5 %all-to-all-start.3 = ((bf16[16,8,4096]{2,1,0:T(8,128)(2,1)}), bf16[16,8,4096]{2,1,0:T(8,128)(2,1)S(1)}, u32[]{:S(2)}, u32[]{:S(2)}) async-start(bf16[16,8,4096]{2,1,0:T(8,128)(2,1)} %bitcast.102), calls=%async_computation.5 | async-start | bytes 2097152 | tf_op jit(solution)/shard_map/all_to_all | solution.py:91
Sparse Core Ops, SparseCore 0:
  135.4 13.4 all-gather.2
  247.8 12.0 all-gather.4
  267.2 12.7 reduce-scatter.2
  282.7 12.1 reduce-scatter.4
where the time goes:
time: 703 us
  waiting for transfers between devices  606 us (86%)
  starting transfers between devices  26.9 us (4%)
  matrix products  22.5 us (3%)
  other arithmetic  17.6 us (3%)
  local copies, waits for them, and re-layouts  15.3 us (2%)
  between operations  14.7 us (2%)
    all_to_all x2, waiting for transfers between devices, on_device(): lax.all_to_all(result, 'expert', split_axis=0, concat_axis=0, tiled=True)  384 us
    all_to_all x2, waiting for transfers between devices, on_device(): lax.all_to_all(send, 'expert', split_axis=0, concat_axis=0, tiled=True)  216 us
    dot_general x2, matrix products, expert_hidden(): jnp.einsum('rd,gdf->grf', rows, gate_up, preferred_element_type=jnp.float32)  17.1 us
  transfers between devices with their start and end apart: 12, of which 6 were waited for; matrix products, arithmetic and copies ran while one was open for 6% of the time, Pallas kernels for 0%

commit v1 on v0

--- a/solution.py
+++ b/solution.py
@@ -88,7 +88,15 @@
             tiled=True,
         )
         result = summed.reshape(slots, cap, width)
-        back = lax.all_to_all(result, "expert", split_axis=0, concat_axis=0, tiled=True)
+        ways, here_2 = (lax.axis_size("expert"), lax.axis_index("expert"))
+        width_2 = result.shape[0] // ways
+        turned = jnp.roll(result, -here_2 * width_2, axis=0)
+        got = [lax.slice_in_dim(turned, 0, width_2, axis=0)]
+        for far in range(1, ways):
+            sent = lax.slice_in_dim(turned, far * width_2, (far + 1) * width_2, axis=0)
+            got.append(lax.ppermute(sent, "expert", [(d, (d + far) % ways) for d in range(ways)]))
+        line = jnp.concatenate(got[::-1], axis=0)
+        back = jnp.roll(line, (here_2 + 1) * got[0].shape[0], axis=0)
         picked = back.reshape(-1, width)[jnp.minimum(slot_index, slots * cap - 1)]
         factor = route_weights[step].reshape(-1) * flat_live.astype(jnp.float32)
         mixed_step = jnp.sum(

time: 703 us -> 738 us (1.050)
  starting transfers between devices: 26.9 us -> 68.3 us
  waiting for transfers between devices: 606 us -> 589 us
    all_to_all x2 -> x0, waiting for transfers between devices: 384 us -> none  [on_device(): lax.all_to_all(result, 'expert', split_axis=0, concat_axis=0, tiled=True)]
    ppermute x4, waiting for transfers between devices: 0.01 us -> 361 us  [partner(): lax.ppermute(x, axis, [(i, i ^ 1 << distance) for i in range(lax.axis_siz...]
    ppermute x0 -> x30, starting transfers between devices: none -> 53.9 us  [on_device(): lax.ppermute(sent, 'expert', [(d, (d + far) % ways) for d in range(ways)])]
    all_to_all x2 -> x0, starting transfers between devices: 12.6 us -> none  [on_device(): lax.all_to_all(result, 'expert', split_axis=0, concat_axis=0, tiled=True)]
    ppermute x0 -> x30, waiting for transfers between devices: none -> 11.7 us  [on_device(): lax.ppermute(sent, 'expert', [(d, (d + far) % ways) for d in range(ways)])]
  transfers between devices with their start and end apart: 12 -> 40, of which waited for: 6 -> 9; matrix products, arithmetic and copies ran while one was open for 6% -> 6% of each run, Pallas kernels for 0% -> 0%
where the time goes in v1:
time: 738 us; the launch traced here: 732 us
  waiting for transfers between devices  589 us (80%)
  starting transfers between devices  68.3 us (9%)
  matrix products  22.5 us (3%)
  other arithmetic  21.5 us (3%)
  local copies, waits for them, and re-layouts  15.6 us (2%)
  between operations  14.9 us (2%)
    ppermute x4, waiting for transfers between devices, partner(): lax.ppermute(x, axis, [(i, i ^ 1 << distance) for i in range(lax.axis_siz...  361 us
    all_to_all x2, waiting for transfers between devices, on_device(): lax.all_to_all(send, 'expert', split_axis=0, concat_axis=0, tiled=True)  217 us
    ppermute x30, starting transfers between devices, on_device(): lax.ppermute(sent, 'expert', [(d, (d + far) % ways) for d in range(ways)])  53.9 us
    dot_general x2, matrix products, expert_hidden(): jnp.einsum('rd,gdf->grf', rows, gate_up, preferred_element_type=jnp.float32)  17.2 us
  transfers between devices with their start and end apart: 40, of which 9 were waited for; matrix products, arithmetic and copies ran while one was open for 6% of the time, Pallas kernels for 0%

profile of v1, /device:TPU:17, one launch (start us, length us, event | category | flops | bytes accessed | tf_op | source)
XLA Modules:
  0.0 731.9 jit_solution(5793999605969523999)
XLA Ops:
  7.2 0.7 broadcast_compare_fusion.1
  8.3 0.7 fusion.65
  10.1 1.1 fusion.42
  11.2 1.0 fusion.44
  12.3 2.4 scatter_custom_fusion
  14.6 6.6 all-to-all-start
  21.4 113.7 %all-to-all-done = bf16[16,8,4096]{2,1,0:T(8,128)(2,1)S(1)} async-done(((bf16[16,8,4096]{2,1,0:T(8,128)(2,1)}), bf16[16,8,4096]{2,1,0:T(8,128)(2,1)S(1)}, u32[]{:S(2)}, u32[]{:S(2)}) %all-to-all-start) | async-done | bytes 1048608 | tf_op jit(solution)/shard_map/all_to_all | solution.py:79
  135.1 1.0 copy-done.2
  136.1 2.4 scatter_custom_fusion.1
  138.5 4.8 all-to-all-start.1
  143.4 0.6 fusion.52
  144.7 102.8 %all-to-all-done.1 = bf16[16,8,4096]{2,1,0:T(8,128)(2,1)S(1)} async-done(((bf16[16,8,4096]{2,1,0:T(8,128)(2,1)}), bf16[16,8,4096]{2,1,0:T(8,128)(2,1)S(1)}, u32[]{:S(2)}, u32[]{:S(2)}) %all-to-all-start.1) | async-done | bytes 1048608 | tf_op jit(solution)/shard_map/all_to_all | solution.py:79
  247.5 1.0 copy-done.1
  248.6 0.7 broadcast_in_dim.19
  249.3 0.9 copy-done.9
  250.2 8.1 %fusion.10 = f32[2,256,512]{1,2,0:T(8,128)S(1)} fusion(bf16[32,8,4096]{2,1,0:T(8,128)(2,1)S(1)} %copy-done.9, bf16[1,2,4096,512]{3,2,1,0:T(8,128)(2,1)} %param.17, bf16[1,2,4096,512]{3,2,1,0:T(8,128)(2,1)S(1)} %bitcast.100), kind=kOutput, calls=%fused_computation.27 | convolution fusion | flops 2151677952 | bytes 19922944 | tf_op jit(solution)/shard_map/rd,gdf->grf/dot_general | solution.py:24
  258.4 0.5 broadcast_in_dim.23
  258.9 1.9 copy-done.3
  260.8 2.4 broadcast_select_fusion.1
  263.2 2.0 copy-done.4
  265.2 2.6 convolution_convert_fusion.1
  268.2 9.0 %fusion.15 = f32[2,256,512]{1,2,0:T(8,128)S(1)} fusion(bf16[32,8,4096]{2,1,0:T(8,128)(2,1)} %all-gather.5.cloned.1.call-done, bf16[1,2,4096,512]{3,2,1,0:T(8,128)(2,1)} %param.17, bf16[1,2,4096,512]{3,2,1,0:T(8,128)(2,1)} %bitcast.101), kind=kOutput, calls=%fused_computation.28 | convolution fusion | flops 2151677952 | bytes 19922944 | tf_op jit(solution)/shard_map/rd,gdf->grf/dot_general | solution.py:24
  277.2 2.7 convolution_convert_fusion
  280.0 2.4 collective-permute-start.31
  282.5 360.7 %collective-permute-done.33 = bf16[1,16,4096]{2,1,0:T(8,128)(2,1)S(1)} collective-permute-done((bf16[1,16,4096]{2,1,0:T(8,128)(2,1)S(1)}, bf16[1,16,4096]{2,1,0:T(8,128)(2,1)S(1)}, u32[]{:S(2)}, u32[]{:S(2)}) %collective-permute-start.33) | collective-permute-done | bytes 131104 | tf_op jit(solution)/shard_map/ppermute | solution.py:10
  643.3 0.7 broadcast_select_fusion.3
  643.9 0.7 broadcast_select_fusion.2
  644.7 1.6 fusion.25
  646.4 4.7 collective-permute-start
  651.0 0.7 collective-permute-start.1
  652.2 5.1 collective-permute-start.3
  657.2 1.6 fusion.22
  658.8 0.7 collective-permute-start.4
  659.6 7.3 broadcast_select_fusion
  667.0 2.6 collective-permute-start.6
  669.9 3.3 collective-permute-start.8
  673.2 0.6 collective-permute-start.9
  673.8 2.6 collective-permute-start.10
  676.5 0.8 collective-permute-start.11
  677.2 3.5 collective-permute-start.12
  680.8 1.7 collective-permute-start.13
  682.5 2.9 collective-permute-start.14
  685.4 1.7 collective-permute-start.15
  687.5 1.5 collective-permute-done.13
  689.0 4.6 collective-permute-start.18
  693.7 3.0 collective-permute-start.19
  696.8 1.5 collective-permute-start.21
  698.3 1.1 collective-permute-start.22
  699.4 3.2 collective-permute-start.23
  702.6 1.0 collective-permute-start.24
  703.6 2.4 collective-permute-start.25
  706.0 1.3 collective-permute-done.21
  707.3 4.1 collective-permute-done.22
  711.5 4.8 collective-permute-start.28
  716.4 1.2 collective-permute-done.27
  717.6 0.6 collective-permute-done.28
  718.2 3.0 collective-permute-done.29
  721.3 0.4 fusion.24
  721.7 0.4 fusion.21
  722.1 0.9 gather_fusion
  722.9 0.5 fusion.27
  723.4 0.9 gather_fusion.1
  724.3 0.5 fusion.26
  724.7 0.7 pad_maximum_fusion
  (124 shorter events, 4.3 us)
Async XLA Ops:
  7.2 136.2 %copy-start.10 = (s32[8]{0:T(128)S(1)}, s32[8]{0:T(128)}, u32[]{:S(2)}) copy-start(s32[8]{0:T(128)} %param.21) | copy-start | bytes 100
  12.2 236.4 %copy-start.6 = (bf16[1,2,128,512]{3,2,1,0:T(8,128)(2,1)S(1)}, bf16[1,2,128,512]{3,2,1,0:T(8,128)(2,1)}, u32[]{:S(2)}) copy-start(bf16[1,2,128,512]{3,2,1,0:T(8,128)(2,1)} %param.18) | copy-start | bytes 786436
  14.6 120.4 %all-to-all-start = ((bf16[16,8,4096]{2,1,0:T(8,128)(2,1)}), bf16[16,8,4096]{2,1,0:T(8,128)(2,1)S(1)}, u32[]{:S(2)}, u32[]{:S(2)}) async-start(bf16[16,8,4096]{2,1,0:T(8,128)(2,1)} %bitcast.8), calls=%async_computation | async-start | bytes 2097152 | tf_op jit(solution)/shard_map/all_to_all | solution.py:79
  21.2 227.4 %all-gather.3.cloned.1.call-start = ((), (), s32[]{:S(2)}) async-start(), calls=%async_computation.4 | async-start | bytes 3145728 | tf_op jit(solution)/shard_map/all_gather | solution.py:80
  21.2 237.1 %collective-permute-start.32 = (bf16[1,512,4096]{2,1,0:T(8,128)(2,1)}, bf16[1,512,4096]{2,1,0:T(8,128)(2,1)}, u32[]{:S(2)}, u32[]{:S(2)}) collective-permute-start(bf16[1,512,4096]{2,1,0:T(8,128)(2,1)} %param.19), channel_id=1, source_target_pairs={{0,16},{2,18},{4,20},{6,22},{8,24},{10,26},{12,28},{14,30},{16,0},... | collective-permute-start | bytes 12582920 | tf_op jit(solution)/shard_map/ppermute | solution.py:10
  135.1 1.0 copy-start.2
  138.5 109.0 %all-to-all-start.1 = ((bf16[16,8,4096]{2,1,0:T(8,128)(2,1)}), bf16[16,8,4096]{2,1,0:T(8,128)(2,1)S(1)}, u32[]{:S(2)}, u32[]{:S(2)}) async-start(bf16[16,8,4096]{2,1,0:T(8,128)(2,1)} %bitcast.27), calls=%async_computation.2 | async-start | bytes 2097152 | tf_op jit(solution)/shard_map/all_to_all | solution.py:79
  143.3 124.8 %all-gather.5.cloned.1.call-start = ((), (), s32[]{:S(2)}) async-start(), calls=%async_computation.6 | async-start | bytes 3145728 | tf_op jit(solution)/shard_map/all_gather | solution.py:80
  247.5 1.0 copy-start.1
  248.5 396.2 %reduce-scatter.3.cloned.1.call-start = ((), (), s32[]{:S(2)}) async-start(), calls=%async_computation.5 | async-start | bytes 3145728 | tf_op jit(solution)/shard_map/reduce_scatter | solution.py:84
  248.6 1.6 copy-start.9
  249.3 9.0 %copy-start = (bf16[2,128,32,512]{3,2,1,0:T(8,128)(2,1)}, bf16[2,128,32,512]{3,2,1,0:T(8,128)(2,1)S(1)}, u32[]{:S(2)}) copy-start(bf16[2,128,32,512]{3,2,1,0:T(8,128)(2,1)S(1)} %broadcast_in_dim.19) | copy-start | bytes 25165828
  250.2 8.2 %copy-start.7 = (bf16[1,16,4096]{2,1,0:T(8,128)(2,1)S(1)}, bf16[1,16,4096]{2,1,0:T(8,128)(2,1)}, u32[]{:S(2)}) copy-start(bf16[1,16,4096]{2,1,0:T(8,128)(2,1)} %param.20) | copy-start | bytes 393220
  258.3 2.5 copy-start.3
  263.2 2.0 copy-start.4
  267.8 389.4 %reduce-scatter.5.cloned.1.call-start = ((), (), s32[]{:S(2)}) async-start(), calls=%async_computation.7 | async-start | bytes 3145728 | tf_op jit(solution)/shard_map/reduce_scatter | solution.py:84
  268.0 390.8 %collective-permute-start.30 = (bf16[1,2,4096,512]{3,2,1,0:T(8,128)(2,1)}, bf16[1,2,4096,512]{3,2,1,0:T(8,128)(2,1)}, u32[]{:S(2)}, u32[]{:S(2)}) collective-permute-start(bf16[1,2,4096,512]{3,2,1,0:T(8,128)(2,1)} %param.17), channel_id=1, source_target_pairs={{0,16},{2,18},{4,20},{6,22},{8,24},{10,26},{12,28},{14,30},{16,0},... | collective-permute-start | bytes 25165832 | tf_op jit(solution)/shard_map/ppermute | solution.py:10
  268.2 9.1 %copy-start.5 = (bf16[1,512,4096]{2,1,0:T(8,128)(2,1)S(1)}, bf16[1,512,4096]{2,1,0:T(8,128)(2,1)}, u32[]{:S(2)}) copy-start(bf16[1,512,4096]{2,1,0:T(8,128)(2,1)} %copy-done.4) | copy-start | bytes 12582916
  277.2 5.2 copy-start.8
  280.0 364.0 %collective-permute-start.31 = (bf16[1,2,128,512]{3,2,1,0:T(8,128)(2,1)S(1)}, bf16[1,2,128,512]{3,2,1,0:T(8,128)(2,1)S(1)}, u32[]{:S(2)}, u32[]{:S(2)}) collective-permute-start(bf16[1,2,128,512]{3,2,1,0:T(8,128)(2,1)S(1)} %copy-done.6), channel_id=1, source_target_pairs={{0,16},{2,18},{4,20},{6,22},{8,24},{10,26},{12,28},{14,30},{16,0},... | collective-permute-start | bytes 786440 | tf_op jit(solution)/shard_map/ppermute | solution.py:10
  282.4 360.9 %collective-permute-start.33 = (bf16[1,16,4096]{2,1,0:T(8,128)(2,1)S(1)}, bf16[1,16,4096]{2,1,0:T(8,128)(2,1)S(1)}, u32[]{:S(2)}, u32[]{:S(2)}) collective-permute-start(bf16[1,16,4096]{2,1,0:T(8,128)(2,1)S(1)} %copy-done.7), channel_id=1, source_target_pairs={{0,16},{2,18},{4,20},{6,22},{8,24},{10,26},{12,28},{14,30},{16,0},... | collective-permute-start | bytes 393224 | tf_op jit(solution)/shard_map/ppermute | solution.py:10
  646.4 20.5 %collective-permute-start = (bf16[1,8,4096]{2,1,0:T(8,128)(2,1)S(1)}, bf16[1,8,4096]{2,1,0:T(8,128)(2,1)S(1)}, u32[]{:S(2)}, u32[]{:S(2)}) collective-permute-start(bf16[1,8,4096]{2,1,0:T(8,128)(2,1)S(1)} %get-tuple-element.28), channel_id=1, source_target_pairs={{0,30},{2,0},{4,2},{6,4},{8,6},{10,8},{12,10},{14,12},{16,14},{18,... | collective-permute-start | bytes 196616 | tf_op jit(solution)/shard_map/ppermute | solution.py:97
  651.0 15.9 %collective-permute-start.1 = (bf16[1,8,4096]{2,1,0:T(8,128)(2,1)S(1)}, bf16[1,8,4096]{2,1,0:T(8,128)(2,1)S(1)}, u32[]{:S(2)}, u32[]{:S(2)}) collective-permute-start(bf16[1,8,4096]{2,1,0:T(8,128)(2,1)S(1)} %get-tuple-element.27), channel_id=1, source_target_pairs={{0,28},{2,30},{4,0},{6,2},{8,4},{10,6},{12,8},{14,10},{16,12},{18,... | collective-permute-start | bytes 196616 | tf_op jit(solution)/shard_map/ppermute | solution.py:97
  651.8 17.8 %collective-permute-start.2 = (bf16[1,8,4096]{2,1,0:T(8,128)(2,1)S(1)}, bf16[1,8,4096]{2,1,0:T(8,128)(2,1)S(1)}, u32[]{:S(2)}, u32[]{:S(2)}) collective-permute-start(bf16[1,8,4096]{2,1,0:T(8,128)(2,1)S(1)} %get-tuple-element.26), channel_id=1, source_target_pairs={{0,26},{2,28},{4,30},{6,0},{8,2},{10,4},{12,6},{14,8},{16,10},{18,... | collective-permute-start | bytes 196616 | tf_op jit(solution)/shard_map/ppermute | solution.py:97
  652.2 17.8 %collective-permute-start.3 = (bf16[1,8,4096]{2,1,0:T(8,128)(2,1)S(1)}, bf16[1,8,4096]{2,1,0:T(8,128)(2,1)S(1)}, u32[]{:S(2)}, u32[]{:S(2)}) collective-permute-start(bf16[1,8,4096]{2,1,0:T(8,128)(2,1)S(1)} %get-tuple-element.25), channel_id=1, source_target_pairs={{0,24},{2,26},{4,28},{6,30},{8,0},{10,2},{12,4},{14,6},{16,8},{18,... | collective-permute-start | bytes 196616 | tf_op jit(solution)/shard_map/ppermute | solution.py:97
  658.8 14.4 %collective-permute-start.4 = (bf16[1,8,4096]{2,1,0:T(8,128)(2,1)S(1)}, bf16[1,8,4096]{2,1,0:T(8,128)(2,1)S(1)}, u32[]{:S(2)}, u32[]{:S(2)}) collective-permute-start(bf16[1,8,4096]{2,1,0:T(8,128)(2,1)S(1)} %get-tuple-element.24), channel_id=1, source_target_pairs={{0,22},{2,24},{4,26},{6,28},{8,30},{10,0},{12,2},{14,4},{16,6},{18... | collective-permute-start | bytes 196616 | tf_op jit(solution)/shard_map/ppermute | solution.py:97
  666.9 6.9 collective-permute-start.5
  667.0 9.5 %collective-permute-start.6 = (bf16[1,8,4096]{2,1,0:T(8,128)(2,1)S(1)}, bf16[1,8,4096]{2,1,0:T(8,128)(2,1)S(1)}, u32[]{:S(2)}, u32[]{:S(2)}) collective-permute-start(bf16[1,8,4096]{2,1,0:T(8,128)(2,1)S(1)} %get-tuple-element.22), channel_id=1, source_target_pairs={{0,18},{2,20},{4,22},{6,24},{8,26},{10,28},{12,30},{14,0},{16,2},{... | collective-permute-start | bytes 196616 | tf_op jit(solution)/shard_map/ppermute | solution.py:97
  669.6 7.6 %collective-permute-start.7 = (bf16[1,8,4096]{2,1,0:T(8,128)(2,1)S(1)}, bf16[1,8,4096]{2,1,0:T(8,128)(2,1)S(1)}, u32[]{:S(2)}, u32[]{:S(2)}) collective-permute-start(bf16[1,8,4096]{2,1,0:T(8,128)(2,1)S(1)} %get-tuple-element.21), channel_id=1, source_target_pairs={{0,16},{2,18},{4,20},{6,22},{8,24},{10,26},{12,28},{14,30},{16,0},... | collective-permute-start | bytes 196616 | tf_op jit(solution)/shard_map/ppermute | solution.py:97
  669.9 10.9 %collective-permute-start.8 = (bf16[1,8,4096]{2,1,0:T(8,128)(2,1)S(1)}, bf16[1,8,4096]{2,1,0:T(8,128)(2,1)S(1)}, u32[]{:S(2)}, u32[]{:S(2)}) collective-permute-start(bf16[1,8,4096]{2,1,0:T(8,128)(2,1)S(1)} %get-tuple-element.20), channel_id=1, source_target_pairs={{0,14},{2,16},{4,18},{6,20},{8,22},{10,24},{12,26},{14,28},{16,30}... | collective-permute-start | bytes 196616 | tf_op jit(solution)/shard_map/ppermute | solution.py:97
  673.2 9.2 %collective-permute-start.9 = (bf16[1,8,4096]{2,1,0:T(8,128)(2,1)S(1)}, bf16[1,8,4096]{2,1,0:T(8,128)(2,1)S(1)}, u32[]{:S(2)}, u32[]{:S(2)}) collective-permute-start(bf16[1,8,4096]{2,1,0:T(8,128)(2,1)S(1)} %get-tuple-element.19), channel_id=1, source_target_pairs={{0,12},{2,14},{4,16},{6,18},{8,20},{10,22},{12,24},{14,26},{16,28}... | collective-permute-start | bytes 196616 | tf_op jit(solution)/shard_map/ppermute | solution.py:97
  673.8 11.6 %collective-permute-start.10 = (bf16[1,8,4096]{2,1,0:T(8,128)(2,1)S(1)}, bf16[1,8,4096]{2,1,0:T(8,128)(2,1)S(1)}, u32[]{:S(2)}, u32[]{:S(2)}) collective-permute-start(bf16[1,8,4096]{2,1,0:T(8,128)(2,1)S(1)} %get-tuple-element.18), channel_id=1, source_target_pairs={{0,10},{2,12},{4,14},{6,16},{8,18},{10,20},{12,22},{14,24},{16,26}... | collective-permute-start | bytes 196616 | tf_op jit(solution)/shard_map/ppermute | solution.py:97
  676.5 10.6 %collective-permute-start.11 = (bf16[1,8,4096]{2,1,0:T(8,128)(2,1)S(1)}, bf16[1,8,4096]{2,1,0:T(8,128)(2,1)S(1)}, u32[]{:S(2)}, u32[]{:S(2)}) collective-permute-start(bf16[1,8,4096]{2,1,0:T(8,128)(2,1)S(1)} %get-tuple-element.17), channel_id=1, source_target_pairs={{0,8},{2,10},{4,12},{6,14},{8,16},{10,18},{12,20},{14,22},{16,24},... | collective-permute-start | bytes 196616 | tf_op jit(solution)/shard_map/ppermute | solution.py:97
  677.2 10.2 %collective-permute-start.12 = (bf16[1,8,4096]{2,1,0:T(8,128)(2,1)S(1)}, bf16[1,8,4096]{2,1,0:T(8,128)(2,1)S(1)}, u32[]{:S(2)}, u32[]{:S(2)}) collective-permute-start(bf16[1,8,4096]{2,1,0:T(8,128)(2,1)S(1)} %get-tuple-element.16), channel_id=1, source_target_pairs={{0,6},{2,8},{4,10},{6,12},{8,14},{10,16},{12,18},{14,20},{16,22},{... | collective-permute-start | bytes 196616 | tf_op jit(solution)/shard_map/ppermute | solution.py:97
  680.8 8.3 %collective-permute-start.13 = (bf16[1,8,4096]{2,1,0:T(8,128)(2,1)S(1)}, bf16[1,8,4096]{2,1,0:T(8,128)(2,1)S(1)}, u32[]{:S(2)}, u32[]{:S(2)}) collective-permute-start(bf16[1,8,4096]{2,1,0:T(8,128)(2,1)S(1)} %get-tuple-element.15), channel_id=1, source_target_pairs={{0,4},{2,6},{4,8},{6,10},{8,12},{10,14},{12,16},{14,18},{16,20},{1... | collective-permute-start | bytes 196616 | tf_op jit(solution)/shard_map/ppermute | solution.py:97
  682.5 11.2 %collective-permute-start.14 = (bf16[1,8,4096]{2,1,0:T(8,128)(2,1)S(1)}, bf16[1,8,4096]{2,1,0:T(8,128)(2,1)S(1)}, u32[]{:S(2)}, u32[]{:S(2)}) collective-permute-start(bf16[1,8,4096]{2,1,0:T(8,128)(2,1)S(1)} %get-tuple-element.14), channel_id=1, source_target_pairs={{0,2},{2,4},{4,6},{6,8},{8,10},{10,12},{12,14},{14,16},{16,18},{18... | collective-permute-start | bytes 196616 | tf_op jit(solution)/shard_map/ppermute | solution.py:97
  685.4 11.3 %collective-permute-start.15 = (bf16[1,8,4096]{2,1,0:T(8,128)(2,1)S(1)}, bf16[1,8,4096]{2,1,0:T(8,128)(2,1)S(1)}, u32[]{:S(2)}, u32[]{:S(2)}) collective-permute-start(bf16[1,8,4096]{2,1,0:T(8,128)(2,1)S(1)} %get-tuple-element.43), channel_id=1, source_target_pairs={{0,30},{2,0},{4,2},{6,4},{8,6},{10,8},{12,10},{14,12},{16,14},{18,... | collective-permute-start | bytes 196616 | tf_op jit(solution)/shard_map/ppermute | solution.py:97
  687.1 9.7 %collective-permute-start.16 = (bf16[1,8,4096]{2,1,0:T(8,128)(2,1)S(1)}, bf16[1,8,4096]{2,1,0:T(8,128)(2,1)S(1)}, u32[]{:S(2)}, u32[]{:S(2)}) collective-permute-start(bf16[1,8,4096]{2,1,0:T(8,128)(2,1)S(1)} %get-tuple-element.42), channel_id=1, source_target_pairs={{0,28},{2,30},{4,0},{6,2},{8,4},{10,6},{12,8},{14,10},{16,12},{18,... | collective-permute-start | bytes 196616 | tf_op jit(solution)/shard_map/ppermute | solution.py:97
  687.5 10.9 %collective-permute-start.17 = (bf16[1,8,4096]{2,1,0:T(8,128)(2,1)S(1)}, bf16[1,8,4096]{2,1,0:T(8,128)(2,1)S(1)}, u32[]{:S(2)}, u32[]{:S(2)}) collective-permute-start(bf16[1,8,4096]{2,1,0:T(8,128)(2,1)S(1)} %get-tuple-element.41), channel_id=1, source_target_pairs={{0,26},{2,28},{4,30},{6,0},{8,2},{10,4},{12,6},{14,8},{16,10},{18,... | collective-permute-start | bytes 196616 | tf_op jit(solution)/shard_map/ppermute | solution.py:97
  689.0 10.4 %collective-permute-start.18 = (bf16[1,8,4096]{2,1,0:T(8,128)(2,1)S(1)}, bf16[1,8,4096]{2,1,0:T(8,128)(2,1)S(1)}, u32[]{:S(2)}, u32[]{:S(2)}) collective-permute-start(bf16[1,8,4096]{2,1,0:T(8,128)(2,1)S(1)} %get-tuple-element.40), channel_id=1, source_target_pairs={{0,24},{2,26},{4,28},{6,30},{8,0},{10,2},{12,4},{14,6},{16,8},{18,... | collective-permute-start | bytes 196616 | tf_op jit(solution)/shard_map/ppermute | solution.py:97
  693.7 9.0 %collective-permute-start.19 = (bf16[1,8,4096]{2,1,0:T(8,128)(2,1)S(1)}, bf16[1,8,4096]{2,1,0:T(8,128)(2,1)S(1)}, u32[]{:S(2)}, u32[]{:S(2)}) collective-permute-start(bf16[1,8,4096]{2,1,0:T(8,128)(2,1)S(1)} %get-tuple-element.39), channel_id=1, source_target_pairs={{0,22},{2,24},{4,26},{6,28},{8,30},{10,0},{12,2},{14,4},{16,6},{18... | collective-permute-start | bytes 196616 | tf_op jit(solution)/shard_map/ppermute | solution.py:97
  696.7 6.9 collective-permute-start.20
  696.8 10.5 %collective-permute-start.21 = (bf16[1,8,4096]{2,1,0:T(8,128)(2,1)S(1)}, bf16[1,8,4096]{2,1,0:T(8,128)(2,1)S(1)}, u32[]{:S(2)}, u32[]{:S(2)}) collective-permute-start(bf16[1,8,4096]{2,1,0:T(8,128)(2,1)S(1)} %get-tuple-element.37), channel_id=1, source_target_pairs={{0,18},{2,20},{4,22},{6,24},{8,26},{10,28},{12,30},{14,0},{16,2},{... | collective-permute-start | bytes 196616 | tf_op jit(solution)/shard_map/ppermute | solution.py:97
  698.3 13.0 %collective-permute-start.22 = (bf16[1,8,4096]{2,1,0:T(8,128)(2,1)S(1)}, bf16[1,8,4096]{2,1,0:T(8,128)(2,1)S(1)}, u32[]{:S(2)}, u32[]{:S(2)}) collective-permute-start(bf16[1,8,4096]{2,1,0:T(8,128)(2,1)S(1)} %get-tuple-element.36), channel_id=1, source_target_pairs={{0,16},{2,18},{4,20},{6,22},{8,24},{10,26},{12,28},{14,30},{16,0},... | collective-permute-start | bytes 196616 | tf_op jit(solution)/shard_map/ppermute | solution.py:97
  699.4 12.0 %collective-permute-start.23 = (bf16[1,8,4096]{2,1,0:T(8,128)(2,1)S(1)}, bf16[1,8,4096]{2,1,0:T(8,128)(2,1)S(1)}, u32[]{:S(2)}, u32[]{:S(2)}) collective-permute-start(bf16[1,8,4096]{2,1,0:T(8,128)(2,1)S(1)} %get-tuple-element.35), channel_id=1, source_target_pairs={{0,14},{2,16},{4,18},{6,20},{8,22},{10,24},{12,26},{14,28},{16,30}... | collective-permute-start | bytes 196616 | tf_op jit(solution)/shard_map/ppermute | solution.py:97
  702.6 13.7 %collective-permute-start.24 = (bf16[1,8,4096]{2,1,0:T(8,128)(2,1)S(1)}, bf16[1,8,4096]{2,1,0:T(8,128)(2,1)S(1)}, u32[]{:S(2)}, u32[]{:S(2)}) collective-permute-start(bf16[1,8,4096]{2,1,0:T(8,128)(2,1)S(1)} %get-tuple-element.34), channel_id=1, source_target_pairs={{0,12},{2,14},{4,16},{6,18},{8,20},{10,22},{12,24},{14,26},{16,28}... | collective-permute-start | bytes 196616 | tf_op jit(solution)/shard_map/ppermute | solution.py:97
  703.6 12.8 %collective-permute-start.25 = (bf16[1,8,4096]{2,1,0:T(8,128)(2,1)S(1)}, bf16[1,8,4096]{2,1,0:T(8,128)(2,1)S(1)}, u32[]{:S(2)}, u32[]{:S(2)}) collective-permute-start(bf16[1,8,4096]{2,1,0:T(8,128)(2,1)S(1)} %get-tuple-element.33), channel_id=1, source_target_pairs={{0,10},{2,12},{4,14},{6,16},{8,18},{10,20},{12,22},{14,24},{16,26}... | collective-permute-start | bytes 196616 | tf_op jit(solution)/shard_map/ppermute | solution.py:97
  707.3 9.1 %collective-permute-start.26 = (bf16[1,8,4096]{2,1,0:T(8,128)(2,1)S(1)}, bf16[1,8,4096]{2,1,0:T(8,128)(2,1)S(1)}, u32[]{:S(2)}, u32[]{:S(2)}) collective-permute-start(bf16[1,8,4096]{2,1,0:T(8,128)(2,1)S(1)} %get-tuple-element.32), channel_id=1, source_target_pairs={{0,8},{2,10},{4,12},{6,14},{8,16},{10,18},{12,20},{14,22},{16,24},... | collective-permute-start | bytes 196616 | tf_op jit(solution)/shard_map/ppermute | solution.py:97
  711.3 6.2 collective-permute-start.27
  711.5 6.8 collective-permute-start.28
  716.3 5.0 collective-permute-start.29
Sparse Core Ops, SparseCore 0:
  136.2 13.4 all-gather.2
  248.6 12.0 all-gather.4
  267.9 12.7 reduce-scatter.2
  283.4 12.1 reduce-scatter.4
